TPU v7x, 256 devices: a whole 4x4x8 slice. The times are simulated.
256 devices in a mesh: batch: 2 (over y_lo), tm: 64 (over z, x, y_hi), mp: 2 (over core).
Axes of the slice: x: 4, y: 4 (y_hi: 2, y_lo: 2; y = y_hi * 2 + y_lo), z: 8, core: 2. Of those that a mesh axis runs over, the one named last changes fastest.
Arguments:
- input_signal: bfloat16 [2, 8192, 1536], P('batch', 'tm'), may hold values from -6 to 6
- standardize_factor: float32 [1536], replicated, may hold values from 0.1 to 1.9
- triple_projection: bfloat16 [3, 1536, 768], P(None, None, 'mp'), may hold values from -0.15625 to 0.15625
- score_sharpening: float32 [8], P('mp'), may hold values from 1 to 3.5
- final_projection: bfloat16 [768, 1536], P('mp'), may hold values from -0.21875 to 0.21875
- filter_taps: float32 [31, 1536], replicated, may hold values from -1.2 to 1.2
- mixture_adjoint: bfloat16 [2, 8192, 1536], P('batch', 'tm'), may hold values from -16 to 16
Outputs:
- sublayer_result: bfloat16 [2, 8192, 1536], P('batch', 'tm')
- signal_adjoint: bfloat16 [2, 8192, 1536], P('batch', 'tm')
- filter_adjoint: float32 [31, 1536], P(None, ('batch', 'tm'))
- amplifier_adjoint: float32 [1536], P(('batch', 'tm'))
All inputs are finite; a program needn't handle non-finite values.
Results may differ from a plain program's by a relative error of at most 0.015.
Values may be sent and summed in bfloat16 or wider, within the bound.
No kernel may reach another device: no remote copies, remote signals or barrier semaphores. Data moves between devices by JAX's collectives and lax.ppermute only.
A program may use at most 128 MiB of HBM per device.

v0:
```python
import math
import jax
import jax.numpy as jnp
from jax import lax
from jax.sharding import PartitionSpec as P

KERNEL = 31


def extended(cells, sides, width):
    for axis, dim in sides:
        count = lax.axis_size(axis)
        ends = count - 1
        head = lax.slice_in_dim(cells, 0, width, axis=dim)
        tail = lax.slice_in_dim(cells, cells.shape[dim] - width, cells.shape[dim], axis=dim)
        cells = jnp.concatenate(
            [
                lax.ppermute(tail, axis, [(i, (i + 1) % count) for i in range(ends)]),
                cells,
                lax.ppermute(head, axis, [((i + 1) % count, i) for i in range(ends)]),
            ],
            axis=dim,
        )
    return cells


def time_rims(field):
    return extended(field, (("tm", 1),), KERNEL // 2)


def heads_total(partial_sum):
    return lax.psum(partial_sum.astype(jnp.bfloat16), "mp").astype(jnp.float32)


def unit_rows(values_in):
    radius = jnp.sqrt(jnp.mean(values_in * values_in, axis=-1, keepdims=True) + 1e-06)
    return (values_in / radius, radius)


def local(
    input_signal,
    standardize_factor,
    triple_projection,
    score_sharpening,
    final_projection,
    filter_taps,
    mixture_adjoint,
):
    rows = input_signal.shape[1]
    resident_subspaces = score_sharpening.shape[0]
    head_breadth = triple_projection.shape[2] // resident_subspaces
    flat_width = resident_subspaces * head_breadth
    taps = filter_taps.shape[0]
    reach = taps // 2
    inputs = input_signal[0].astype(jnp.float32)
    centred = inputs - jnp.mean(inputs, axis=-1, keepdims=True)
    variance = jnp.mean(centred * centred, axis=-1, keepdims=True)
    inverse_std = 1.0 / jnp.sqrt(variance + 1e-05)
    incoming_entries = centred * inverse_std
    normed = (incoming_entries * standardize_factor).astype(jnp.bfloat16)
    query = jnp.dot(normed, triple_projection[0], preferred_element_type=jnp.float32).reshape(
        rows, resident_subspaces, head_breadth
    )
    key_raw = jnp.dot(normed, triple_projection[1], preferred_element_type=jnp.float32).reshape(
        rows, resident_subspaces, head_breadth
    )
    value_raw = jnp.dot(normed, triple_projection[2], preferred_element_type=jnp.float32).reshape(
        rows, resident_subspaces, head_breadth
    )
    normalized_probes, q_radius = unit_rows(query)
    khat, k_radius = unit_rows(key_raw)
    head_sharpening = (score_sharpening / math.sqrt(head_breadth))[None, :, None]
    probe_vectors = (normalized_probes * head_sharpening).astype(jnp.bfloat16)
    keys_local = khat.astype(jnp.bfloat16)
    values_local = value_raw.astype(jnp.bfloat16)
    incoming_adjoint = mixture_adjoint[0].astype(jnp.float32)
    grad_pad = time_rims(mixture_adjoint)[0].astype(jnp.float32)
    grad_res = incoming_adjoint
    for tap_index in range(taps):
        grad_res = (
            grad_res
            + filter_taps[tap_index]
            * grad_pad[2 * reach - tap_index : 2 * reach - tap_index + rows]
        )
    grad_heads = jnp.dot(
        grad_res.astype(jnp.bfloat16), final_projection.T, preferred_element_type=jnp.float32
    )
    grad_heads = grad_heads.astype(jnp.bfloat16).reshape(rows, resident_subspaces, head_breadth)
    zeros_rows = jnp.zeros((rows, resident_subspaces), jnp.float32)
    zeros_full = jnp.zeros((rows, resident_subspaces, head_breadth), jnp.float32)
    start_state = (zeros_rows, zeros_full, zeros_rows, zeros_full, zeros_full)
    key_flat = keys_local.reshape(rows, flat_width)
    value_flat = values_local.reshape(rows, flat_width)
    carry = start_state
    key_piece = lax.all_gather(key_flat, "tm", axis=0, tiled=True)
    value_piece = lax.all_gather(value_flat, "tm", axis=0, tiled=True)
    piece_rows = key_piece.shape[0]
    block_rows = math.gcd(piece_rows, 512)
    block_count = piece_rows // block_rows
    key_blocks = key_piece.reshape(block_count, block_rows, resident_subspaces, head_breadth)
    value_blocks = value_piece.reshape(block_count, block_rows, resident_subspaces, head_breadth)

    def step(state, blocks):
        totals, numer, expect, first, second = state
        key_block, value_block = blocks
        score = jnp.einsum(
            "qhe,khe->qhk", probe_vectors, key_block, preferred_element_type=jnp.float32
        )
        weight = jnp.exp(score)
        weight_low = weight.astype(jnp.bfloat16)
        numer = numer + jnp.einsum(
            "qhk,khe->qhe", weight_low, value_block, preferred_element_type=jnp.float32
        )
        product = jnp.einsum(
            "qhe,khe->qhk", grad_heads, value_block, preferred_element_type=jnp.float32
        )
        weighted = weight * product
        first = first + jnp.einsum(
            "qhk,khe->qhe",
            weighted.astype(jnp.bfloat16),
            key_block,
            preferred_element_type=jnp.float32,
        )
        second = second + jnp.einsum(
            "qhk,khe->qhe", weight_low, key_block, preferred_element_type=jnp.float32
        )
        totals = totals + jnp.sum(weight, axis=-1)
        expect = expect + jnp.sum(weighted, axis=-1)
        return ((totals, numer, expect, first, second), None)

    carry, _ = lax.scan(step, carry, (key_blocks, value_blocks))
    totals, numer, expect, first, second = carry
    attended = (numer / totals[..., None]).astype(jnp.bfloat16)
    deltas = expect / totals
    probe_sensitivity = (first - deltas[..., None] * second) / totals[..., None]
    partial_out = jnp.dot(
        attended.reshape(rows, flat_width), final_projection, preferred_element_type=jnp.float32
    )
    residual = (inputs + heads_total(partial_out)).astype(jnp.bfloat16)
    res_pad = time_rims(residual[None])[0].astype(jnp.float32)
    sublayer_result = residual.astype(jnp.float32)
    filter_pieces = []
    for tap_index in range(taps):
        receptive_span = res_pad[tap_index : tap_index + rows]
        sublayer_result = sublayer_result + filter_taps[tap_index] * receptive_span
        filter_pieces.append(jnp.sum(incoming_adjoint * receptive_span, axis=0))
    sublayer_result = sublayer_result.astype(jnp.bfloat16)
    filter_terms = jnp.stack(filter_pieces)
    carry = (zeros_full, zeros_full)
    query_piece = lax.all_gather(probe_vectors.reshape(rows, flat_width), "tm", axis=0, tiled=True)
    grad_piece = lax.all_gather(grad_heads.reshape(rows, flat_width), "tm", axis=0, tiled=True)
    total_piece = lax.all_gather(totals.astype(jnp.bfloat16), "tm", axis=0, tiled=True).astype(
        jnp.float32
    )
    delta_piece = lax.all_gather(deltas.astype(jnp.bfloat16), "tm", axis=0, tiled=True).astype(
        jnp.float32
    )
    piece_rows = query_piece.shape[0]
    block_rows = math.gcd(piece_rows, 512)
    block_count = piece_rows // block_rows
    query_blocks = query_piece.reshape(block_count, block_rows, resident_subspaces, head_breadth)
    grad_blocks = grad_piece.reshape(block_count, block_rows, resident_subspaces, head_breadth)
    total_blocks = total_piece.reshape(block_count, block_rows, resident_subspaces)
    delta_blocks = delta_piece.reshape(block_count, block_rows, resident_subspaces)

    def step(state, blocks):
        key_sum, value_sum = state
        query_block, grad_block, total_block, delta_block = blocks
        score = jnp.einsum(
            "khe,qhe->khq", keys_local, query_block, preferred_element_type=jnp.float32
        )
        prob = jnp.exp(score) / total_block.T[None]
        value_sum = value_sum + jnp.einsum(
            "khq,qhe->khe",
            prob.astype(jnp.bfloat16),
            grad_block,
            preferred_element_type=jnp.float32,
        )
        product = jnp.einsum(
            "khe,qhe->khq", values_local, grad_block, preferred_element_type=jnp.float32
        )
        slope = prob * (product - delta_block.T[None])
        key_sum = key_sum + jnp.einsum(
            "khq,qhe->khe",
            slope.astype(jnp.bfloat16),
            query_block,
            preferred_element_type=jnp.float32,
        )
        return ((key_sum, value_sum), None)

    carry, _ = lax.scan(step, carry, (query_blocks, grad_blocks, total_blocks, delta_blocks))
    grad_keys, grad_values = carry
    sharpened_sensitivity = probe_sensitivity * head_sharpening
    query_grad = (
        sharpened_sensitivity
        - normalized_probes
        * jnp.mean(sharpened_sensitivity * normalized_probes, axis=-1, keepdims=True)
    ) / q_radius
    key_grad = (grad_keys - khat * jnp.mean(grad_keys * khat, axis=-1, keepdims=True)) / k_radius
    normed_part = jnp.dot(
        query_grad.astype(jnp.bfloat16).reshape(rows, flat_width),
        triple_projection[0].T,
        preferred_element_type=jnp.float32,
    )
    normed_part = normed_part + jnp.dot(
        key_grad.astype(jnp.bfloat16).reshape(rows, flat_width),
        triple_projection[1].T,
        preferred_element_type=jnp.float32,
    )
    normed_part = normed_part + jnp.dot(
        grad_values.astype(jnp.bfloat16).reshape(rows, flat_width),
        triple_projection[2].T,
        preferred_element_type=jnp.float32,
    )
    standardized_adjoint = heads_total(normed_part)
    amplifier_terms = jnp.sum(standardized_adjoint * incoming_entries, axis=0)
    scaled = standardized_adjoint * standardize_factor
    frame_back = (
        scaled
        - jnp.mean(scaled, axis=-1, keepdims=True)
        - incoming_entries * jnp.mean(scaled * incoming_entries, axis=-1, keepdims=True)
    ) * inverse_std
    signal_adjoint = (grad_res + frame_back).astype(jnp.bfloat16)
    kernel_part, gain_part = (
        lax.psum_scatter(filter_terms, ("batch", "tm"), scatter_dimension=1, tiled=True),
        lax.psum_scatter(amplifier_terms, ("batch", "tm"), scatter_dimension=0, tiled=True),
    )
    return (sublayer_result[None], signal_adjoint[None], kernel_part, gain_part)


def solution(mesh):
    return jax.shard_map(
        local,
        mesh=mesh,
        in_specs=(
            P("batch", "tm", None),
            P(),
            P(None, None, "mp"),
            P("mp"),
            P("mp", None),
            P(),
            P("batch", "tm", None),
        ),
        out_specs=(
            P("batch", "tm", None),
            P("batch", "tm", None),
            P(None, ("batch", "tm")),
            P(("batch", "tm")),
        ),
        check_vma=False,
    )
```

profile of v0, /device:TPU:2, one launch (start us, length us, event | category | flops | bytes accessed | tf_op | source)
XLA Modules:
  0.0 1526.4 jit_solution(12637345963958603732)
XLA Ops:
  9.7 3.8 slice_bitcast_fusion
  13.5 2.4 copy.43
  19.2 2.4 copy.45
  21.7 2.5 convolution_convert_fusion.2
  28.5 5.1 collective-permute-start
  33.6 3.1 collective-permute-start.1
  37.7 3.6 collective-permute-done.1
  41.4 3.1 fusion.132
  46.6 94.8 %all-gather.5.cloned.1.call-done = bf16[8192,384]{0,1:T(8,128)(2,1)} async-done(((bf16[128,384]{0,1:T(8,128)(2,1)}), bf16[8192,384]{0,1:T(8,128)(2,1)}) %all-gather.5.cloned.1.call-update) | async-done | bytes 6291472 | tf_op jit(solution)/shard_map/all_gather | solution.py:95
  141.4 5.7 copy.62
  147.1 6.3 copy.47
  153.5 111.7 %all-gather.7.cloned.1.call-done = bf16[8192,384]{0,1:T(8,128)(2,1)} async-done(((bf16[128,384]{0,1:T(8,128)(2,1)}), bf16[8192,384]{0,1:T(8,128)(2,1)}) %all-gather.7.cloned.1.call-update) | async-done | bytes 6291472 | tf_op jit(solution)/shard_map/all_gather | solution.py:96
  265.1 5.7 copy.63
  270.8 16.8 %copy.48 = bf16[16,512,4,96]{1,3,2,0:T(8,128)(2,1)} copy(bf16[16,512,4,96]{1,0,3,2:T(8,128)(2,1)S(1)} %bitcast.714) | data formatting | bytes 12582912
  287.6 128.9 %while.32 = (s32[]{:T(128)}, f32[128,4]{0,1:T(4,128)S(1)}, f32[128,4,96]{0,2,1:T(8,128)}, f32[128,4]{0,1:T(4,128)S(1)}, f32[128,4,96]{0,2,1:T(8,128)}, /*index=5...) while((s32[]{:T(128)}, f32[128,4]{0,1:T(4,128)S(1)}, ...), condition=%wide.region_7.8_spmd.clone, body=%wide.region_4.7_spmd.clone.sunk | while | flops 253527040 | bytes 8997542 | solution.py:131
  290.4 1.9 fusion.231
  293.6 1.9 fusion.230
  298.3 2.0 fusion.231
  301.6 2.0 fusion.230
  306.4 2.0 fusion.231
  309.7 2.0 fusion.230
  314.4 2.0 fusion.231
  317.7 2.0 fusion.230
  322.5 2.0 fusion.231
  325.8 2.0 fusion.230
  330.5 2.0 fusion.231
  333.8 2.0 fusion.230
  338.6 2.0 fusion.231
  341.9 2.0 fusion.230
  346.6 2.0 fusion.231
  350.0 2.0 fusion.230
  354.7 2.0 fusion.231
  358.0 2.0 fusion.230
  362.8 2.0 fusion.231
  366.1 2.0 fusion.230
  370.9 2.0 fusion.231
  374.2 2.0 fusion.230
  379.0 2.0 fusion.231
  382.3 2.0 fusion.230
  387.1 2.0 fusion.231
  390.4 2.0 fusion.230
  395.1 2.0 fusion.231
  398.4 2.0 fusion.230
  403.2 2.0 fusion.231
  406.5 2.0 fusion.230
  411.2 2.0 fusion.231
  414.5 2.0 fusion.230
  416.5 177.8 %all_gather.21 = bf16[8192,4]{0,1:T(4,128)(2,1)S(1)} all-gather(bf16[128,4]{0,1:T(4,128)(2,1)S(1)} %get-tuple-element.367), channel_id=1, replica_groups=mesh['batch'=2,'tm'=64,'mp'=2] {'tm'}, dimensions={0}, use_global_device_ids=true | all-gather | bytes 66560 | tf_op jit(solution)/shard_map/all_gather | solution.py:152
  594.4 174.2 %all_gather.23 = bf16[8192,4]{0,1:T(4,128)(2,1)S(1)} all-gather(bf16[128,4]{0,1:T(4,128)(2,1)S(1)} %get-tuple-element.348), channel_id=1, replica_groups=mesh['batch'=2,'tm'=64,'mp'=2] {'tm'}, dimensions={0}, use_global_device_ids=true | all-gather | bytes 66560 | tf_op jit(solution)/shard_map/all_gather | solution.py:155
  768.6 5.7 copy.64
  774.4 6.4 copy.50
  783.9 16.0 %reshape.263 = bf16[16,512,4,96]{3,2,1,0:T(4,128)(2,1)} reshape(bf16[8192,384]{1,0:T(8,128)(2,1)} %all-gather.11.cloned.1.call-done) | data formatting | bytes 12582912 | tf_op jit(solution)/shard_map/reshape | solution.py:162
  800.0 13.3 copy.51
  813.2 75.2 %while.33 = (s32[]{:T(128)}, f32[128,4,96]{0,2,1:T(8,128)S(1)}, f32[128,4,96]{0,2,1:T(8,128)S(1)}, bf16[16,512,4,96]{1,3,2,0:T(8,128)(2,1)}, bf16[128,4,96]{0,2,...) while((s32[]{:T(128)}, f32[128,4,96]{0,2,1:T(8,128)S(1)}, ...), condition=%wide.region_11.12_spmd.clone, body=%wide.region_10.11_spmd.clone.sunk | while | flops 202833920 | bytes 5752956 | solution.py:191
  890.5 2.5 fusion.48
  893.2 30.2 %all-reduce.8.cloned.1.call-done = (bf16[128,1536]{1,0:T(8,128)(2,1)}, bf16[128,1536]{1,0:T(8,128)(2,1)}) async-done(((bf16[128,1536]{1,0:T(8,128)(2,1)}, bf16[128,1536]{1,0:T(8,128)(2,1)}), (bf16[128,1536]{1,0:T(8,128)(2,1)}, bf16[128,1536]{1,0:T(8,128)(2,1)})) %all-reduce.8.cloned.1.call-update) | async-done | bytes 786448 | tf_op jit(solution)/shard_map/psum | solution.py:32
  924.9 2.3 fusion.168
  927.2 4.9 collective-permute-start.2
  932.1 3.3 collective-permute-start.3
  936.7 349.4 %all-reduce.1 = f32[1536]{0:T(1024)S(1)} all-reduce(f32[1536]{0:T(1024)S(1)} %get-tuple-element.274), channel_id=3, replica_groups=mesh['batch'=2,'tm'=64,'mp'=2] {'batch','tm'}, use_global_device_ids=true, to_apply=%region_49.50.clone | all-reduce | flops 1536 | bytes 12288
  1286.8 2.0 fusion.130
  1290.6 2.7 stack.127
  1293.7 4.7 fusion.170
  1298.4 219.4 %all-reduce.6.cloned.1.call-done = f32[31,1536]{1,0:T(8,128)} async-done(((f32[31,1536]{1,0:T(8,128)}), f32[31,1536]{1,0:T(8,128)}) %all-reduce.6.cloned.1.call-update) | async-done | bytes 190480
  (437 shorter events, 163.2 us)
Async XLA Ops:
  7.2 37.7 %copy-start = (bf16[384,1536]{1,0:T(8,128)(2,1)S(1)}, bf16[384,1536]{1,0:T(8,128)(2,1)}, u32[]{:S(2)}) copy-start(bf16[384,1536]{1,0:T(8,128)(2,1)} %param.15) | copy-start | bytes 3538948
  7.2 134.2 %all-gather.5.cloned.1.call-start = ((), (), s32[]{:S(2)}) async-start(), calls=%async_computation | async-start | bytes 6389760 | tf_op jit(solution)/shard_map/all_gather | solution.py:95
  8.5 17.4 %copy-start.86 = (f32[128]{0:T(128)}, f32[128]{0:T(128)S(1)}, u32[]{:S(2)}) copy-start(f32[128]{0:T(128)S(1)} %broadcast_multiply_fusion.5) | copy-start | bytes 1540
  9.7 16.1 %copy-start.88 = (f32[128]{0:T(128)}, f32[128]{0:T(128)S(1)}, u32[]{:S(2)}) copy-start(f32[128]{0:T(128)S(1)} %add_rsqrt_fusion) | copy-start | bytes 1540
  18.5 7.3 copy-start.90
  19.2 246.0 %all-gather.7.cloned.1.call-start = ((), (), s32[]{:S(2)}) async-start(), calls=%async_computation.1 | async-start | bytes 6389760 | tf_op jit(solution)/shard_map/all_gather | solution.py:96
  21.6 6.9 copy-start.4
  21.6 15.1 copy-start.20
  24.2 744.4 %all-gather.9.cloned.1.call-start = ((), (), s32[]{:S(2)}) async-start(), calls=%async_computation.2 | async-start | bytes 6389760 | tf_op jit(solution)/shard_map/all_gather | solution.py:150
  27.7 13.8 copy-start.13
  28.4 755.5 %all-gather.11.cloned.1.call-start = ((), (), s32[]{:S(2)}) async-start(), calls=%async_computation.3 | async-start | bytes 6389760 | tf_op jit(solution)/shard_map/all_gather | solution.py:151
  28.5 9.2 collective-permute-start
  33.6 7.7 collective-permute-start.1
  37.1 7.4 copy-start.21
  37.1 7.4 copy-start.23
  37.1 7.4 copy-start.25
  37.2 7.4 copy-start.27
  37.2 7.4 copy-start.29
  37.2 7.4 copy-start.31
  37.2 7.4 copy-start.33
  37.2 7.4 copy-start.35
  37.2 7.4 copy-start.37
  37.2 7.4 copy-start.39
  37.2 7.4 copy-start.41
  37.2 7.4 copy-start.43
  37.2 7.4 copy-start.45
  37.3 7.4 copy-start.47
  37.3 7.4 copy-start.49
  37.3 7.4 copy-start.51
  37.3 7.4 copy-start.53
  37.3 7.4 copy-start.55
  37.3 7.4 copy-start.57
  37.5 7.2 copy-start.59
  37.5 7.2 copy-start.61
  37.5 7.2 copy-start.63
  37.5 7.2 copy-start.65
  37.6 7.2 copy-start.67
  37.6 7.2 copy-start.69
  37.6 7.2 copy-start.71
  37.6 7.2 copy-start.73
  37.6 7.2 copy-start.74
  37.6 7.2 copy-start.75
  37.6 7.2 copy-start.76
  37.6 7.2 copy-start.77
  44.9 102.3 %copy-start.8 = (f32[128,1536]{1,0:T(8,128)}, f32[128,1536]{1,0:T(8,128)S(1)}, u32[]{:S(2)}) copy-start(f32[128,1536]{1,0:T(8,128)S(1)} %fusion.132) | copy-start | bytes 2359300
  46.2 877.3 %all-reduce.8.cloned.1.call-start = ((), (), s32[]{:S(2)}) async-start(), calls=%async_computation.5 | async-start | bytes 1572864 | tf_op jit(solution)/shard_map/psum | solution.py:32
  270.8 16.8 %copy-start.10 = (bf16[128,4,96]{0,2,1:T(8,128)(2,1)S(1)}, bf16[128,4,96]{0,2,1:T(8,128)(2,1)}, u32[]{:S(2)}) copy-start(bf16[128,4,96]{0,2,1:T(8,128)(2,1)} %multiply_convert_fusion) | copy-start | bytes 294916
  774.3 6.4 copy-start.3
  774.4 6.5 copy-start.7
  799.9 13.3 copy-start.6
  799.9 13.3 copy-start.12
  799.9 13.3 copy-start.19
  813.2 75.2 %copy-start.16 = (f32[128,4,96]{0,2,1:T(8,128)S(1)}, f32[128,4,96]{0,2,1:T(8,128)}, u32[]{:S(2)}) copy-start(f32[128,4,96]{0,2,1:T(8,128)} %copy-done.15) | copy-start | bytes 589828
  813.2 75.2 %copy-start.81 = (f32[128,4]{0,1:T(4,128)S(1)}, f32[128,4]{0,1:T(4,128)}, u32[]{:S(2)}) copy-start(f32[128,4]{0,1:T(4,128)} %copy-done.80) | copy-start | bytes 6148
  888.5 35.0 %copy-start.79 = (f32[1536]{0:T(1024)S(1)}, f32[1536]{0:T(1024)}, u32[]{:S(2)}) copy-start(f32[1536]{0:T(1024)} %param.12) | copy-start | bytes 18436
  888.5 35.0 %copy-start.87 = (f32[128]{0:T(128)S(1)}, f32[128]{0:T(128)}, u32[]{:S(2)}) copy-start(f32[128]{0:T(128)} %copy-done.86) | copy-start | bytes 1540
  888.5 35.0 %copy-start.89 = (f32[128]{0:T(128)S(1)}, f32[128]{0:T(128)}, u32[]{:S(2)}) copy-start(f32[128]{0:T(128)} %copy-done.88) | copy-start | bytes 1540
  888.6 36.3 %copy-start.9 = (f32[128,1536]{1,0:T(8,128)S(1)}, f32[128,1536]{1,0:T(8,128)}, u32[]{:S(2)}) copy-start(f32[128,1536]{1,0:T(8,128)} %copy-done.8) | copy-start | bytes 2359300
  890.4 45.0 %copy-start.91 = (u32[256]{0:T(256)S(1)}, u32[256]{0:T(256)}, u32[]{:S(2)}) copy-start(u32[256]{0:T(256)} %constant.50) | copy-start | bytes 3076
  893.0 393.8 %copy-start.5 = (bf16[1,128,1536]{2,1,0:T(8,128)(2,1)S(1)}, bf16[1,128,1536]{2,1,0:T(8,128)(2,1)}, u32[]{:S(2)}) copy-start(bf16[1,128,1536]{2,1,0:T(8,128)(2,1)} %param.17) | copy-start | bytes 1179652
  893.0 624.8 %all-reduce.6.cloned.1.call-start = ((), (), s32[]{:S(2)}) async-start(), calls=%async_computation.4 | async-start | bytes 393216
  927.2 359.5 %collective-permute-start.2 = (bf16[1,15,1536]{2,1,0:T(8,128)(2,1)S(1)}, bf16[1,15,1536]{2,1,0:T(8,128)(2,1)S(1)}, u32[]{:S(2)}, u32[]{:S(2)}) collective-permute-start(bf16[1,15,1536]{2,1,0:T(8,128)(2,1)S(1)} %get-tuple-element.363), channel_id=1, source_target_pairs={{0,2},{2,4},{4,6},{6,8},{8,10},{10,12},{12,14},{14,16},{16,18},{18... | collective-permute-start | bytes 138248 | tf_op jit(solution)/shard_map/ppermute | solution.py:18
  932.1 354.5 %collective-permute-start.3 = (bf16[1,15,1536]{2,1,0:T(8,128)(2,1)S(1)}, bf16[1,15,1536]{2,1,0:T(8,128)(2,1)S(1)}, u32[]{:S(2)}, u32[]{:S(2)}) collective-permute-start(bf16[1,15,1536]{2,1,0:T(8,128)(2,1)S(1)} %get-tuple-element.364), channel_id=1, source_target_pairs={{2,0},{4,2},{6,4},{8,6},{10,8},{12,10},{14,12},{16,14},{18,16},{20... | collective-permute-start | bytes 138248 | tf_op jit(solution)/shard_map/ppermute | solution.py:20
  1293.7 225.6 %copy-start.1 = (bf16[384,1536]{1,0:T(8,128)(2,1)S(1)}, bf16[384,1536]{1,0:T(8,128)(2,1)}, u32[]{:S(2)}) copy-start(bf16[384,1536]{1,0:T(8,128)(2,1)} %param.15) | copy-start | bytes 3538948
  (53 other events, 217.2 us)
Sparse Core Ops, SparseCore 0:
  19.3 122.1 all-gather.4
  144.9 120.2 all-gather.6
  268.6 120.2 all-gather.8
  392.4 138.0 all-gather.10
  893.1 30.2 all-reduce.7
  1293.5 224.1 all-reduce.5
where the time goes:
time: 1540 us; the launch traced here: 1530 us
  blocking collectives  701 us (46%)
  waiting for transfers between devices  460 us (30%)
  matrix products  217 us (14%)
  local copies, waits for them, and re-layouts  94.1 us (6%)
  other arithmetic  19.3 us (1%)
  starting transfers between devices  17.3 us (1%)
  between operations  16.8 us (1%)
    unnamed x1, blocking collectives  349 us
    unnamed x7, waiting for transfers between devices  219 us
    all_gather x1, blocking collectives, local(): lax.all_gather(totals.astype(jnp.bfloat16), 'tm', axis=0, tiled=True)  178 us
    all_gather x1, blocking collectives, local(): lax.all_gather(deltas.astype(jnp.bfloat16), 'tm', axis=0, tiled=True)  174 us
    all_gather x1, waiting for transfers between devices, local(): value_piece = lax.all_gather(value_flat, 'tm', axis=0, tiled=True)  112 us
    all_gather x1, waiting for transfers between devices, local(): key_piece = lax.all_gather(key_flat, 'tm', axis=0, tiled=True)  94.8 us
    unnamed x193, local copies, waits for them, and re-layouts  63.6 us
    dot_general x16, matrix products, step(): jnp.einsum('qhk,khe->qhe', weight_low, value_block, preferred_element_typ...  31.8 us
  transfers between devices with their start and end apart: 10, of which 5 were waited for; matrix products, arithmetic and copies ran while one was open for 13% of the time, Pallas kernels for 0%

commit v1 on v0

--- a/solution.py
+++ b/solution.py
@@ -5,6 +5,12 @@
 from jax.sharding import PartitionSpec as P
 
 KERNEL = 31
+
+
+def _recover_frames(z_in, t0, axis_id):
+    formed = jnp.concatenate([z_in, t0], 1)
+    opened = lax.all_gather(formed, axis_id, axis=0, tiled=True)
+    return jnp.split(opened, [z_in.shape[1]], 1)
 
 
 def extended(cells, sides, width):
@@ -92,8 +98,7 @@
     key_flat = keys_local.reshape(rows, flat_width)
     value_flat = values_local.reshape(rows, flat_width)
     carry = start_state
-    key_piece = lax.all_gather(key_flat, "tm", axis=0, tiled=True)
-    value_piece = lax.all_gather(value_flat, "tm", axis=0, tiled=True)
+    key_piece, value_piece = _recover_frames(key_flat, value_flat, axis_id="tm")
     piece_rows = key_piece.shape[0]
     block_rows = math.gcd(piece_rows, 512)
     block_count = piece_rows // block_rows

time: 1540 us -> 1690 us (1.097)
  waiting for transfers between devices: 460 us -> 609 us
    all_gather x1, waiting for transfers between devices: 0.02 us -> 130 us  [local(): lax.all_gather(grad_heads.reshape(rows, flat_width), 'tm', axis=0, tiled=...]
    all_gather x1, waiting for transfers between devices: 0.02 us -> 92.6 us  [local(): lax.all_gather(probe_vectors.reshape(rows, flat_width), 'tm', axis=0, til...]
    all_gather x2 -> x1, waiting for transfers between devices: 206 us -> 126 us  [_recover_frames(): opened = lax.all_gather(formed, axis_id, axis=0, tiled=True)]
    unnamed x193 -> x177, local copies, waits for them, and re-layouts: 63.6 us -> 50.3 us
    unnamed x7 -> x6, waiting for transfers between devices: 219 us -> 224 us
  transfers between devices with their start and end apart: 10 -> 9, of which waited for: 5 -> 6; matrix products, arithmetic and copies ran while one was open for 13% -> 4% of each run, Pallas kernels for 0% -> 0%
where the time goes in v1:
time: 1690 us; the launch traced here: 1680 us
  blocking collectives  697 us (41%)
  waiting for transfers between devices  609 us (36%)
  matrix products  217 us (13%)
  local copies, waits for them, and re-layouts  101 us (6%)
  other arithmetic  20.8 us (1%)
    unnamed x1, blocking collectives  347 us
    unnamed x6, waiting for transfers between devices  224 us
    all_gather x1, blocking collectives, local(): lax.all_gather(totals.astype(jnp.bfloat16), 'tm', axis=0, tiled=True)  176 us
    all_gather x1, blocking collectives, local(): lax.all_gather(deltas.astype(jnp.bfloat16), 'tm', axis=0, tiled=True)  174 us
    all_gather x1, waiting for transfers between devices, local(): lax.all_gather(grad_heads.reshape(rows, flat_width), 'tm', axis=0, tiled=...  130 us
    all_gather x1, waiting for transfers between devices, _recover_frames(): opened = lax.all_gather(formed, axis_id, axis=0, tiled=True)  126 us
    all_gather x1, waiting for transfers between devices, local(): lax.all_gather(probe_vectors.reshape(rows, flat_width), 'tm', axis=0, til...  92.6 us
    unnamed x177, local copies, waits for them, and re-layouts  50.3 us
  transfers between devices with their start and end apart: 9, of which 6 were waited for; matrix products, arithmetic and copies ran while one was open for 4% of the time, Pallas kernels for 0%

profile of v1, /device:TPU:2, one launch (start us, length us, event | category | flops | bytes accessed | tf_op | source)
XLA Modules:
  0.0 1678.3 jit_solution(6459833492583470057)
XLA Ops:
  7.2 3.8 slice_bitcast_fusion
  16.3 5.1 collective-permute-start.1
  21.4 2.3 collective-permute-start
  24.6 5.3 collective-permute-done
  29.9 3.1 fusion.132
  34.6 2.4 copy.44
  37.0 2.5 copy.43
  45.9 92.6 %all-gather.6.cloned.1.call-done = bf16[8192,384]{0,1:T(8,128)(2,1)} async-done(((bf16[128,384]{0,1:T(8,128)(2,1)}), bf16[8192,384]{0,1:T(8,128)(2,1)}) %all-gather.6.cloned.1.call-update) | async-done | bytes 6291472 | tf_op jit(solution)/shard_map/all_gather | solution.py:155
  138.5 5.7 copy.64
  144.2 6.3 copy.50
  150.6 129.5 %all-gather.8.cloned.1.call-done = bf16[8192,384]{1,0:T(8,128)(2,1)} async-done(((bf16[128,384]{1,0:T(8,128)(2,1)}), bf16[8192,384]{1,0:T(8,128)(2,1)}) %all-gather.8.cloned.1.call-update) | async-done | bytes 6291472 | tf_op jit(solution)/shard_map/all_gather | solution.py:156
  280.1 16.0 reshape.263
  296.1 13.2 copy.51
  309.2 126.5 %all-gather.4.cloned.1.call-done = bf16[8192,768]{0,1:T(8,128)(2,1)} async-done(((bf16[128,768]{0,1:T(8,128)(2,1)}), bf16[8192,768]{0,1:T(8,128)(2,1)}) %all-gather.4.cloned.1.call-update) | async-done | bytes 12582928 | tf_op jit(solution)/shard_map/all_gather | solution.py:12
  435.7 8.7 fusion.181
  444.4 5.7 copy.62
  450.1 6.3 copy.47
  456.4 2.9 copy.63
  459.4 6.5 copy.48
  465.8 128.6 %while.32 = (s32[]{:T(128)}, f32[128,4]{0,1:T(4,128)S(1)}, f32[128,4,96]{0,2,1:T(8,128)}, f32[128,4]{0,1:T(4,128)S(1)}, f32[128,4,96]{0,2,1:T(8,128)}, /*index=5...) while((s32[]{:T(128)}, f32[128,4]{0,1:T(4,128)S(1)}, ...), condition=%wide.region_7.8_spmd.clone, body=%wide.region_4.7_spmd.clone.sunk | while | flops 253527040 | bytes 8601758 | solution.py:136
  476.6 2.0 fusion.231
  478.6 2.0 fusion.232
  484.6 2.0 fusion.231
  486.6 2.0 fusion.232
  492.7 2.0 fusion.231
  494.7 2.0 fusion.232
  500.7 2.0 fusion.231
  502.7 2.0 fusion.232
  508.7 2.0 fusion.231
  510.7 2.0 fusion.232
  516.8 2.0 fusion.231
  518.8 2.0 fusion.232
  524.8 2.0 fusion.231
  526.8 2.0 fusion.232
  532.9 2.0 fusion.231
  534.9 2.0 fusion.232
  540.9 2.0 fusion.231
  542.9 2.0 fusion.232
  549.0 2.0 fusion.231
  550.9 2.0 fusion.232
  557.0 2.0 fusion.231
  559.0 2.0 fusion.232
  565.0 2.0 fusion.231
  567.0 2.0 fusion.232
  573.1 2.0 fusion.231
  575.1 2.0 fusion.232
  581.1 2.0 fusion.231
  589.2 2.0 fusion.231
  591.2 2.0 fusion.232
  598.0 2.7 fusion.49
  600.7 175.9 %all_gather.17 = bf16[8192,4]{0,1:T(4,128)(2,1)S(1)} all-gather(bf16[128,4]{0,1:T(4,128)(2,1)S(1)} %get-tuple-element.369), channel_id=1, replica_groups=mesh['batch'=2,'tm'=64,'mp'=2] {'tm'}, dimensions={0}, use_global_device_ids=true | all-gather | bytes 66560 | tf_op jit(solution)/shard_map/all_gather | solution.py:157
  776.6 174.2 %all_gather.19 = bf16[8192,4]{0,1:T(4,128)(2,1)S(1)} all-gather(bf16[128,4]{0,1:T(4,128)(2,1)S(1)} %get-tuple-element.348), channel_id=1, replica_groups=mesh['batch'=2,'tm'=64,'mp'=2] {'tm'}, dimensions={0}, use_global_device_ids=true | all-gather | bytes 66560 | tf_op jit(solution)/shard_map/all_gather | solution.py:160
  951.5 86.3 %while.33 = (s32[]{:T(128)}, f32[128,4,96]{0,2,1:T(8,128)S(1)}, f32[128,4,96]{0,2,1:T(8,128)S(1)}, bf16[16,512,4,96]{1,3,2,0:T(8,128)(2,1)}, bf16[128,4,96]{0,2,...) while((s32[]{:T(128)}, f32[128,4,96]{0,2,1:T(8,128)S(1)}, ...), condition=%wide.region_11.12_spmd.clone, body=%wide.region_10.11_spmd.clone.sunk | while | flops 202833920 | bytes 5752459 | solution.py:196
  1038.0 2.1 convolution_add_fusion.1
  1040.1 2.5 fusion.48
  1042.7 31.3 %all-reduce.8.cloned.1.call-done = (bf16[128,1536]{1,0:T(8,128)(2,1)}, bf16[128,1536]{1,0:T(8,128)(2,1)}) async-done(((bf16[128,1536]{1,0:T(8,128)(2,1)}, bf16[128,1536]{1,0:T(8,128)(2,1)}), (bf16[128,1536]{1,0:T(8,128)(2,1)}, bf16[128,1536]{1,0:T(8,128)(2,1)})) %all-reduce.8.cloned.1.call-update) | async-done | bytes 786448 | tf_op jit(solution)/shard_map/psum | solution.py:38
  1075.4 2.3 fusion.168
  1077.7 4.9 collective-permute-start.3
  1082.6 2.4 collective-permute-start.2
  1086.3 347.3 %all-reduce.1 = f32[1536]{0:T(1024)S(1)} all-reduce(f32[1536]{0:T(1024)S(1)} %get-tuple-element.274), channel_id=3, replica_groups=mesh['batch'=2,'tm'=64,'mp'=2] {'batch','tm'}, use_global_device_ids=true, to_apply=%region_49.50.clone | all-reduce | flops 1536 | bytes 12288
  1434.3 2.2 fusion.130
  1438.4 2.7 stack.127
  1441.4 4.6 fusion.170
  1446.0 224.0 %all-reduce.6.cloned.1.call-done = f32[31,1536]{1,0:T(8,128)} async-done(((f32[31,1536]{1,0:T(8,128)}), f32[31,1536]{1,0:T(8,128)}) %all-reduce.6.cloned.1.call-update) | async-done | bytes 190480
  (388 shorter events, 179.7 us)
Async XLA Ops:
  7.2 26.2 %copy-start = (bf16[384,1536]{1,0:T(8,128)(2,1)S(1)}, bf16[384,1536]{1,0:T(8,128)(2,1)}, u32[]{:S(2)}) copy-start(bf16[384,1536]{1,0:T(8,128)(2,1)} %param.15) | copy-start | bytes 3538948
  7.2 5.5 copy-start.1
  7.2 6.4 copy-start.73
  7.2 131.3 %all-gather.6.cloned.1.call-start = ((), (), s32[]{:S(2)}) async-start(), calls=%async_computation.1 | async-start | bytes 6389760 | tf_op jit(solution)/shard_map/all_gather | solution.py:155
  11.1 5.2 copy-start.2
  11.1 12.6 copy-start.15
  12.8 28.7 %copy-start.79 = (f32[128]{0:T(128)}, f32[128]{0:T(128)S(1)}, u32[]{:S(2)}) copy-start(f32[128]{0:T(128)S(1)} %broadcast_multiply_fusion.5) | copy-start | bytes 1540
  15.4 14.5 copy-start.9
  16.3 263.8 %all-gather.8.cloned.1.call-start = ((), (), s32[]{:S(2)}) async-start(), calls=%async_computation.2 | async-start | bytes 6389760 | tf_op jit(solution)/shard_map/all_gather | solution.py:156
  16.3 8.2 collective-permute-start.1
  21.4 8.4 collective-permute-start
  24.0 9.0 copy-start.16
  24.0 9.0 copy-start.18
  24.0 9.0 copy-start.20
  24.1 9.0 copy-start.22
  24.1 9.0 copy-start.24
  24.1 9.0 copy-start.26
  24.1 9.0 copy-start.28
  24.1 9.0 copy-start.30
  24.1 9.0 copy-start.32
  24.1 9.0 copy-start.34
  24.1 9.0 copy-start.36
  24.1 9.0 copy-start.38
  24.1 9.0 copy-start.40
  24.2 9.0 copy-start.42
  24.2 9.0 copy-start.44
  24.2 9.0 copy-start.46
  24.2 9.0 copy-start.48
  24.2 9.0 copy-start.50
  24.2 9.0 copy-start.52
  24.4 8.8 copy-start.54
  24.4 8.8 copy-start.56
  24.4 8.8 copy-start.58
  24.4 8.8 copy-start.60
  24.5 8.8 copy-start.62
  24.5 8.8 copy-start.64
  24.5 8.8 copy-start.66
  24.5 8.8 copy-start.68
  24.5 8.8 copy-start.69
  24.5 8.8 copy-start.70
  24.5 8.8 copy-start.71
  24.5 8.8 copy-start.72
  33.4 8.0 copy-start.5
  34.6 401.1 %all-gather.4.cloned.1.call-start = ((), (), s32[]{:S(2)}) async-start(), calls=%async_computation | async-start | bytes 12779520 | tf_op jit(solution)/shard_map/all_gather | solution.py:12
  37.0 8.1 copy-start.13
  41.4 102.8 %copy-start.10 = (f32[128,4,96]{0,2,1:T(8,128)}, f32[128,4,96]{0,2,1:T(8,128)S(1)}, u32[]{:S(2)}) copy-start(f32[128,4,96]{0,2,1:T(8,128)S(1)} %get-tuple-element.373) | copy-start | bytes 589828
  41.5 102.8 %copy-start.14 = (bf16[128,4,96]{0,2,1:T(8,128)(2,1)}, bf16[128,4,96]{0,2,1:T(8,128)(2,1)S(1)}, u32[]{:S(2)}) copy-start(bf16[128,4,96]{0,2,1:T(8,128)(2,1)S(1)} %fusion.172) | copy-start | bytes 294916
  44.7 1029.2 %all-reduce.8.cloned.1.call-start = ((), (), s32[]{:S(2)}) async-start(), calls=%async_computation.4 | async-start | bytes 1572864 | tf_op jit(solution)/shard_map/psum | solution.py:38
  594.4 357.1 %copy-start.4 = (f32[128,4,96]{0,2,1:T(8,128)S(1)}, f32[128,4,96]{0,2,1:T(8,128)}, u32[]{:S(2)}) copy-start(f32[128,4,96]{0,2,1:T(8,128)} %custom-call.6) | copy-start | bytes 589828
  594.4 357.1 %copy-start.8 = (bf16[128,4,96]{0,2,1:T(8,128)(2,1)S(1)}, bf16[128,4,96]{0,2,1:T(8,128)(2,1)}, u32[]{:S(2)}) copy-start(bf16[128,4,96]{0,2,1:T(8,128)(2,1)} %copy-done.7) | copy-start | bytes 294916
  951.5 86.3 %copy-start.11 = (f32[128,4,96]{0,2,1:T(8,128)S(1)}, f32[128,4,96]{0,2,1:T(8,128)}, u32[]{:S(2)}) copy-start(f32[128,4,96]{0,2,1:T(8,128)} %copy-done.10) | copy-start | bytes 589828
  951.5 86.3 %copy-start.77 = (f32[128,4]{0,1:T(4,128)S(1)}, f32[128,4]{0,1:T(4,128)}, u32[]{:S(2)}) copy-start(f32[128,4]{0,1:T(4,128)} %copy-done.76) | copy-start | bytes 6148
  1037.9 36.1 %copy-start.74 = (f32[1536]{0:T(1024)S(1)}, f32[1536]{0:T(1024)}, u32[]{:S(2)}) copy-start(f32[1536]{0:T(1024)} %param.12) | copy-start | bytes 18436
  1037.9 36.1 %copy-start.80 = (f32[128]{0:T(128)S(1)}, f32[128]{0:T(128)}, u32[]{:S(2)}) copy-start(f32[128]{0:T(128)} %copy-done.79) | copy-start | bytes 1540
  1038.0 37.4 %copy-start.6 = (f32[128,1536]{1,0:T(8,128)S(1)}, f32[128,1536]{1,0:T(8,128)}, u32[]{:S(2)}) copy-start(f32[128,1536]{1,0:T(8,128)} %copy-done.5) | copy-start | bytes 2359300
  1040.1 45.0 %copy-start.82 = (u32[256]{0:T(256)S(1)}, u32[256]{0:T(256)}, u32[]{:S(2)}) copy-start(u32[256]{0:T(256)} %constant.50) | copy-start | bytes 3076
  1042.6 391.7 %copy-start.3 = (bf16[1,128,1536]{2,1,0:T(8,128)(2,1)S(1)}, bf16[1,128,1536]{2,1,0:T(8,128)(2,1)}, u32[]{:S(2)}) copy-start(bf16[1,128,1536]{2,1,0:T(8,128)(2,1)} %param.17) | copy-start | bytes 1179652
  1042.6 627.4 %all-reduce.6.cloned.1.call-start = ((), (), s32[]{:S(2)}) async-start(), calls=%async_computation.3 | async-start | bytes 393216
  1077.7 356.5 %collective-permute-start.3 = (bf16[1,15,1536]{2,1,0:T(8,128)(2,1)S(1)}, bf16[1,15,1536]{2,1,0:T(8,128)(2,1)S(1)}, u32[]{:S(2)}, u32[]{:S(2)}) collective-permute-start(bf16[1,15,1536]{2,1,0:T(8,128)(2,1)S(1)} %get-tuple-element.366), channel_id=1, source_target_pairs={{2,0},{4,2},{6,4},{8,6},{10,8},{12,10},{14,12},{16,14},{18,16},{20... | collective-permute-start | bytes 138248 | tf_op jit(solution)/shard_map/ppermute | solution.py:26
  1082.6 351.6 %collective-permute-start.2 = (bf16[1,15,1536]{2,1,0:T(8,128)(2,1)S(1)}, bf16[1,15,1536]{2,1,0:T(8,128)(2,1)S(1)}, u32[]{:S(2)}, u32[]{:S(2)}) collective-permute-start(bf16[1,15,1536]{2,1,0:T(8,128)(2,1)S(1)} %get-tuple-element.365), channel_id=1, source_target_pairs={{0,2},{2,4},{4,6},{6,8},{8,10},{10,12},{12,14},{14,16},{16,18},{18... | collective-permute-start | bytes 138248 | tf_op jit(solution)/shard_map/ppermute | solution.py:24
  1436.5 4.7 copy-start.12
  1436.5 4.7 copy-start.17
  1436.5 4.7 copy-start.19
  1436.5 4.7 copy-start.21
  (28 other events, 117.7 us)
Sparse Core Ops, SparseCore 0:
  16.4 122.1 all-gather.5
  142.2 137.8 all-gather.7
  283.5 152.1 all-gather.3
  1042.8 31.1 all-reduce.7
  1441.3 228.7 all-reduce.5
